TPU v7x, 256 devices: a whole 4x4x8 slice. The times are simulated.
256 devices in a mesh: fsdp: 32 (over x_hi, z, core), ctx: 8 (over x_lo, y).
Axes of the slice: x: 4 (x_hi: 2, x_lo: 2; x = x_hi * 2 + x_lo), y: 4, z: 8, core: 2. Of those that a mesh axis runs over, the one named last changes fastest.
Arguments:
- hidden: bfloat16 [2048, 8192], P('ctx', 'fsdp'), may hold values from -6 to 6
- gain: bfloat16 [8192], replicated, may hold values from 0.25 to 1.75
- embed: bfloat16 [512, 8192], P(None, 'fsdp'), may hold values from -6 to 6
- qkv_weight: bfloat16 [8192, 12288], P('fsdp'), may hold values from -0.07164475 to 0.07164475
- out_weight: bfloat16 [4096, 8192], P('fsdp'), may hold values from -1 to 1
- ref_ids: int32 [2048], P('ctx'), may hold values from 0 to 511
- var_pos: int32 [128], P('ctx'), may hold values from 0 to 2047, as said below
- var_base: int32 [128], P('ctx'), may hold values from 0 to 511
Outputs:
- mixed: bfloat16 [2, 2048, 8192], P(None, 'ctx', 'fsdp')
Inputs may be any that keep to these rules, and one draw needn't show every extreme that they name: Each block of 256 consecutive positions holds exactly 16 distinct variant positions, and they are listed among that block's 16 entries of var_pos.
All inputs are finite; a program needn't handle non-finite values.
Results may differ from a plain program's by a relative error of at most 0.025.
Values may be sent and summed in bfloat16 or wider, within the bound.
No kernel may reach another device: no remote copies, remote signals or barrier semaphores. Data moves between devices by JAX's collectives and lax.ppermute only.
A program may use at most 128 MiB of HBM per device.

v0:
```python
import jax
import jax.numpy as jnp
from jax import lax
from jax.sharding import PartitionSpec as P

epsilon = 1e-05
rope_base = 10000.0


def from_behind(block, axis, distance):
    devices = range(lax.axis_size(axis))
    route = [(i - distance, i) for i in devices if i - distance in devices]
    return lax.ppermute(block, axis, route)


def rotate(values, positions):
    half = values.shape[-1] // 2
    exponent = jnp.arange(half).astype(jnp.float32) * (-2.0 / values.shape[-1])
    inv_freq = jnp.power(jnp.float32(rope_base), exponent)
    angle = positions.astype(jnp.float32)[:, None] * inv_freq[None, :]
    cosine = jnp.cos(angle)
    sine = jnp.sin(angle)
    first = values[..., :half]
    second = values[..., half:]
    return jnp.concatenate(
        [first * cosine - second * sine, second * cosine + first * sine], axis=-1
    )


def shards(hidden, gain, embed, qkv_weight, out_weight, ref_ids, var_pos, var_base):
    tok_rows, width_part = hidden.shape
    head_size = out_weight.shape[0]
    full_width = out_weight.shape[1]
    vocab_size = embed.shape[0]
    my_block = lax.axis_index("ctx")
    cycle_len = lax.axis_size("ctx")
    local_pos = var_pos - my_block * tok_rows
    var_spots = local_pos[:, None] == jnp.arange(tok_rows)[None, :]
    placer = var_spots.T.astype(jnp.bfloat16)
    changed = jnp.any(var_spots, axis=0)
    ref_at = jnp.sum(jnp.where(var_spots, ref_ids[None, :], 0), axis=1)
    vocab_line = jnp.arange(vocab_size)[None, :]
    onehot_diff = (vocab_line == var_base[:, None]).astype(jnp.bfloat16) - (
        vocab_line == ref_at[:, None]
    ).astype(jnp.bfloat16)
    change = jnp.dot(onehot_diff, embed, preferred_element_type=jnp.float32)
    picked_rows = jnp.dot(
        var_spots.astype(jnp.bfloat16), hidden, preferred_element_type=jnp.float32
    )
    var_rows = (picked_rows + change).astype(jnp.bfloat16)
    placed_rows = jnp.dot(placer, var_rows, preferred_element_type=jnp.float32).astype(jnp.bfloat16)
    variant = jnp.where(changed[:, None], placed_rows, hidden)
    head_w = lax.all_to_all(qkv_weight, "fsdp", split_axis=1, concat_axis=0, tiled=True)
    block_pos = my_block * tok_rows + jnp.arange(tok_rows)

    def finish(proj_rows, positions):
        query_part = rotate(proj_rows[:, :head_size], positions)
        key_part = rotate(proj_rows[:, head_size : 2 * head_size], positions)
        return jnp.concatenate(
            [query_part, key_part, proj_rows[:, 2 * head_size :]], axis=1
        ).astype(jnp.bfloat16)

    dense_rows = jnp.concatenate([hidden, variant], axis=0)
    gain_part = gain.astype(jnp.float32)
    widened = lax.all_gather(dense_rows, "fsdp", axis=1, tiled=True).astype(jnp.float32)
    scaled = (widened * gain_part[None, :]).astype(jnp.bfloat16)
    running = jnp.dot(scaled, head_w, preferred_element_type=jnp.float32)
    running, squares = (running, jnp.sum(widened * widened, axis=1))
    inv_rms = lax.rsqrt(squares / full_width + epsilon)
    proj_all = running * inv_rms[:, None]
    ref_qkv = finish(proj_all[:tok_rows], block_pos)
    var_qkv = finish(proj_all[tok_rows:], block_pos)
    both_qkv = jnp.stack([ref_qkv, var_qkv])
    queries = both_qkv[:, :, :head_size]
    kv_blocks = jnp.stack(
        [both_qkv[:, :, head_size : 2 * head_size], both_qkv[:, :, 2 * head_size :]]
    )
    score_scale = 1.0 / head_size**0.5
    carried = (
        jnp.full((2, tok_rows), -jnp.inf, jnp.float32),
        jnp.zeros((2, tok_rows), jnp.float32),
        jnp.zeros((2, tok_rows, head_size), jnp.float32),
    )
    blocks_now = kv_blocks
    for rotation in range(cycle_len):
        source = my_block - rotation
        attend_top, attend_denom, attend_running = carried
        key_pos = source * tok_rows + jnp.arange(tok_rows)
        visible = (block_pos[:, None] >= key_pos[None, :]) & (source >= 0)
        score = (
            jnp.einsum("sqd,skd->sqk", queries, blocks_now[0], preferred_element_type=jnp.float32)
            * score_scale
        )
        score = jnp.where(visible[None], score, -jnp.inf)
        new_top = jnp.maximum(attend_top, jnp.max(score, axis=-1))
        safe_top = jnp.where(jnp.isfinite(new_top), new_top, 0.0)
        probs = jnp.exp(score - safe_top[..., None])
        factor = jnp.exp(attend_top - safe_top)
        attend_denom = attend_denom * factor + jnp.sum(probs, axis=-1)
        attend_running = attend_running * factor[..., None] + jnp.einsum(
            "sqk,skd->sqd",
            probs.astype(jnp.bfloat16),
            blocks_now[1],
            preferred_element_type=jnp.float32,
        )
        carried = (new_top, attend_denom, attend_running)
        if rotation + 1 < cycle_len:
            blocks_now = from_behind(blocks_now, "ctx", 1)
    top, denom, running = carried
    attn_flat = (running / denom[..., None]).astype(jnp.bfloat16).reshape(2 * tok_rows, head_size)
    branch = lax.psum_scatter(
        lax.dot_general(
            out_weight, attn_flat, (((0,), (1,)), ((), ())), preferred_element_type=jnp.float32
        ).astype(jnp.bfloat16),
        "fsdp",
        scatter_dimension=0,
        tiled=True,
    ).astype(jnp.float32)
    branch = branch.T.reshape(2, tok_rows, width_part)
    seqs = jnp.stack([hidden, variant]).astype(jnp.float32)
    return (seqs + branch).astype(jnp.bfloat16)


def solution(mesh):
    in_specs = (
        P("ctx", "fsdp"),
        P(),
        P(None, "fsdp"),
        P("fsdp", None),
        P("fsdp", None),
        P("ctx"),
        P("ctx"),
        P("ctx"),
    )
    out_specs = P(None, "ctx", "fsdp")
    return jax.shard_map(shards, mesh=mesh, in_specs=in_specs, out_specs=out_specs, check_vma=False)
```

profile of v0, /device:TPU:8, one launch (start us, length us, event | category | flops | bytes accessed | tf_op | source)
XLA Modules:
  0.0 472.9 jit_solution(10370490574901621818)
XLA Ops:
  6.5 0.8 broadcast_subtract_fusion
  7.3 0.1 fusion.108
  7.4 1.1 fusion.107
  8.5 0.9 select_reduce_fusion
  9.4 1.4 fusion.26
  10.8 1.6 pad_maximum_fusion
  12.5 8.6 %copy.107 = bf16[256,12288]{0,1:T(8,128)(2,1)} copy(bf16[256,12288]{1,0:T(8,128)(2,1)} %param.11) | data formatting | bytes 12582912 | tf_op args[3]
  21.0 11.6 %all-to-all-start = ((bf16[256,32,384]{0,2,1:T(8,128)(2,1)}), bf16[256,32,384]{0,2,1:T(8,128)(2,1)}, u32[]{:S(2)}, u32[]{:S(2)}) async-start(bf16[256,32,384]{0,2,1:T(8,128)(2,1)} %bitcast.108), calls=%async_computation | async-start | bytes 12582912 | tf_op jit(solution)/shard_map/all_to_all | solution.py:53
  32.7 161.2 %all-to-all-done = bf16[256,32,384]{0,2,1:T(8,128)(2,1)} async-done(((bf16[256,32,384]{0,2,1:T(8,128)(2,1)}), bf16[256,32,384]{0,2,1:T(8,128)(2,1)}, u32[]{:S(2)}, u32[]{:S(2)}) %all-to-all-start) | async-done | bytes 6291488 | tf_op jit(solution)/shard_map/all_to_all | solution.py:53
  193.9 8.6 %copy.108 = bf16[32,256,384]{2,1,0:T(8,128)(2,1)} copy(bf16[32,256,384]{1,2,0:T(8,128)(2,1)} %bitcast.3) | data formatting | bytes 12582912 | tf_op jit(solution)/shard_map/all_to_all | solution.py:53
  202.5 5.2 %all-gather.2.cloned.1.call-done = bf16[512,8192]{1,0:T(8,128)(2,1)} async-done(((bf16[512,256]{1,0:T(8,128)(2,1)}), bf16[512,8192]{1,0:T(8,128)(2,1)}) %all-gather.2.cloned.1.call-update) | async-done | bytes 8388624 | tf_op jit(solution)/shard_map/all_gather | solution.py:65
  207.8 5.3 %fusion.1 = f32[512]{0:T(512)S(1)} fusion(bf16[512,8192]{1,0:T(8,128)(2,1)} %all-gather.2.cloned.1.call-done), kind=kLoop, calls=%fused_computation.3 | loop fusion | flops 12582400 | bytes 8390656 | tf_op jit(solution)/shard_map/reduce_sum | solution.py:68
  213.1 0.5 copy-done.1
  213.6 7.1 %fusion.115 = (bf16[512,384]{0,1:T(8,128)(2,1)}, f32[512,384]{0,1:T(8,128)S(1)}) fusion(f32[512]{0:T(512)S(1)} %add_rsqrt_fusion, bf16[8192,384]{1,0:T(8,128)(2,1)} %bitcast.109, bf16[512,8192]{1,0:T(8,128)(2,1)S(1)} %copy-done.1, f32[8192]{0:T(1024)S(1)} %convert_element_type.105), kind=kOutput, calls=%fused_computation.200 | convolution fusion | flops 3234201600 | bytes 15894528 | tf_op jit(solution)/shard_map/dot_general | solution.py:67
  220.7 0.3 bitcast_dynamic-update-slice_fusion.3
  221.0 0.3 bitcast_dynamic-update-slice_fusion.2
  221.3 0.3 bitcast_dynamic-update-slice_fusion.1
  221.6 0.3 bitcast_dynamic-update-slice_fusion.6
  221.9 0.3 bitcast_dynamic-update-slice_fusion
  222.3 0.3 bitcast_dynamic-update-slice_fusion.4
  222.6 0.9 fusion.94
  223.5 3.4 collective-permute-start
  226.9 7.0 %collective-permute-done = bf16[2,2,256,128]{2,3,1,0:T(8,128)(2,1)S(1)} collective-permute-done((bf16[2,2,256,128]{2,3,1,0:T(8,128)(2,1)S(1)}, bf16[2,2,256,128]{2,3,1,0:T(8,128)(2,1)S(1)}, u32[]{:S(2)}, u32[]{:S(2)}) %collective-permute-start) | collective-permute-done | bytes 262176 | tf_op jit(solution)/shard_map/ppermute | solution.py:13
  233.9 3.4 collective-permute-start.1
  237.3 6.1 %collective-permute-done.1 = bf16[2,2,256,128]{2,3,1,0:T(8,128)(2,1)S(1)} collective-permute-done((bf16[2,2,256,128]{2,3,1,0:T(8,128)(2,1)S(1)}, bf16[2,2,256,128]{2,3,1,0:T(8,128)(2,1)S(1)}, u32[]{:S(2)}, u32[]{:S(2)}) %collective-permute-start.1) | collective-permute-done | bytes 262176 | tf_op jit(solution)/shard_map/ppermute | solution.py:13
  243.5 3.4 collective-permute-start.2
  246.9 5.2 %collective-permute-done.2 = bf16[2,2,256,128]{2,3,1,0:T(8,128)(2,1)S(1)} collective-permute-done((bf16[2,2,256,128]{2,3,1,0:T(8,128)(2,1)S(1)}, bf16[2,2,256,128]{2,3,1,0:T(8,128)(2,1)S(1)}, u32[]{:S(2)}, u32[]{:S(2)}) %collective-permute-start.2) | collective-permute-done | bytes 262176 | tf_op jit(solution)/shard_map/ppermute | solution.py:13
  252.1 3.4 collective-permute-start.3
  255.5 0.6 compare_and_fusion.6
  256.0 0.3 fusion.122
  256.3 4.0 collective-permute-done.3
  260.3 3.8 collective-permute-start.4
  264.1 0.3 fusion.123
  264.4 0.3 fusion.121
  264.7 4.0 collective-permute-done.4
  268.7 5.8 %collective-permute-start.5 = (bf16[2,2,256,128]{2,3,1,0:T(8,128)(2,1)S(1)}, bf16[2,2,256,128]{2,3,1,0:T(8,128)(2,1)S(1)}, u32[]{:S(2)}, u32[]{:S(2)}) collective-permute-start(bf16[2,2,256,128]{2,3,1,0:T(8,128)(2,1)S(1)} %collective-permute-done.4), channel_id=1, source_target_pairs={{0,1},{1,2},{2,3},{3,4},{4,5},{5,6},{6,7},{8,9},{9,10},{10,11},{11... | collective-permute-start | bytes 786440 | tf_op jit(solution)/shard_map/ppermute | solution.py:13
  274.5 0.3 fusion.120
  274.8 0.3 fusion.119
  275.1 3.3 collective-permute-done.5
  278.4 6.7 %collective-permute-start.6 = (bf16[2,2,256,128]{2,3,1,0:T(8,128)(2,1)S(1)}, bf16[2,2,256,128]{2,3,1,0:T(8,128)(2,1)S(1)}, u32[]{:S(2)}, u32[]{:S(2)}) collective-permute-start(bf16[2,2,256,128]{2,3,1,0:T(8,128)(2,1)S(1)} %collective-permute-done.5), channel_id=1, source_target_pairs={{0,1},{1,2},{2,3},{3,4},{4,5},{5,6},{6,7},{8,9},{9,10},{10,11},{11... | collective-permute-start | bytes 786440 | tf_op jit(solution)/shard_map/ppermute | solution.py:13
  285.0 0.3 fusion.118
  285.3 0.3 fusion.117
  285.6 3.1 collective-permute-done.6
  288.7 0.3 fusion.116
  289.1 0.1 fusion.28
  289.2 0.1 fusion.30
  289.3 0.1 fusion.32
  289.4 0.1 fusion.34
  289.5 0.1 fusion.36
  289.6 0.1 fusion.38
  289.7 0.1 fusion.40
  289.8 0.1 fusion.42
  289.9 0.3 fusion.24
  290.2 0.3 fusion.23
  290.5 0.3 fusion.22
  290.9 1.2 fusion.21
  292.1 0.3 fusion.20
  292.4 0.3 fusion.19
  292.7 0.3 fusion.18
  293.0 0.3 fusion.25
  293.3 5.6 %fusion.2 = bf16[8192,512]{0,1:T(8,128)(2,1)} fusion(bf16[512,128]{1,0:T(8,128)(2,1)S(1)} %bitcast.113, bf16[128,8192]{1,0:T(8,128)(2,1)S(1)} %copy-done), kind=kOutput, calls=%fused_computation.5 | convolution fusion | flops 1077936128 | bytes 10616832 | tf_op jit(solution)/shard_map/dot_general | solution.py:112
  298.9 165.4 %reduce-scatter.2.cloned.1.call-done = bf16[256,512]{0,1:T(8,128)(2,1)} async-done(((bf16[8192,512]{0,1:T(8,128)(2,1)}), bf16[256,512]{0,1:T(8,128)(2,1)}) %reduce-scatter.2.cloned.1.call-update) | async-done | bytes 262160 | tf_op jit(solution)/shard_map/reduce_scatter | solution.py:111
  464.3 1.0 reshape.674
  465.3 0.8 add_convert_fusion
  (31 shorter events, 0.3 us)
Async XLA Ops:
  6.5 286.8 %copy-start = (bf16[128,8192]{1,0:T(8,128)(2,1)S(1)}, bf16[128,8192]{1,0:T(8,128)(2,1)}, u32[]{:S(2)}) copy-start(bf16[128,8192]{1,0:T(8,128)(2,1)} %param.12) | copy-start | bytes 6291460
  6.5 201.2 %all-gather.2.cloned.1.call-start = ((), (), s32[]{:S(2)}) async-start(), calls=%async_computation.2 | async-start | bytes 8650752 | tf_op jit(solution)/shard_map/all_gather | solution.py:65
  21.0 11.6 %copy-start.4 = (bf16[8192]{0:T(1024)(128)(2,1)S(1)}, bf16[8192]{0:T(1024)(128)(2,1)}, u32[]{:S(2)}) copy-start(bf16[8192]{0:T(1024)(128)(2,1)} %param.9) | copy-start | bytes 49156
  21.0 172.9 %all-to-all-start = ((bf16[256,32,384]{0,2,1:T(8,128)(2,1)}), bf16[256,32,384]{0,2,1:T(8,128)(2,1)}, u32[]{:S(2)}, u32[]{:S(2)}) async-start(bf16[256,32,384]{0,2,1:T(8,128)(2,1)} %bitcast.108), calls=%async_computation | async-start | bytes 12582912 | tf_op jit(solution)/shard_map/all_to_all | solution.py:53
  32.6 431.7 %reduce-scatter.2.cloned.1.call-start = ((), (), s32[]{:S(2)}) async-start(), calls=%async_computation.3 | async-start | bytes 8650752 | tf_op jit(solution)/shard_map/reduce_scatter | solution.py:111
  207.8 5.8 %copy-start.1 = (bf16[512,8192]{1,0:T(8,128)(2,1)S(1)}, bf16[512,8192]{1,0:T(8,128)(2,1)}, u32[]{:S(2)}) copy-start(bf16[512,8192]{1,0:T(8,128)(2,1)} %all-gather.2.cloned.1.call-done) | copy-start | bytes 25165828
  223.5 10.4 %collective-permute-start = (bf16[2,2,256,128]{2,3,1,0:T(8,128)(2,1)S(1)}, bf16[2,2,256,128]{2,3,1,0:T(8,128)(2,1)S(1)}, u32[]{:S(2)}, u32[]{:S(2)}) collective-permute-start(bf16[2,2,256,128]{2,3,1,0:T(8,128)(2,1)S(1)} %pad_maximum_fusion.1), channel_id=1, source_target_pairs={{0,1},{1,2},{2,3},{3,4},{4,5},{5,6},{6,7},{8,9},{9,10},{10,11},{11... | collective-permute-start | bytes 786440 | tf_op jit(solution)/shard_map/ppermute | solution.py:13
  233.9 9.5 %collective-permute-start.1 = (bf16[2,2,256,128]{2,3,1,0:T(8,128)(2,1)S(1)}, bf16[2,2,256,128]{2,3,1,0:T(8,128)(2,1)S(1)}, u32[]{:S(2)}, u32[]{:S(2)}) collective-permute-start(bf16[2,2,256,128]{2,3,1,0:T(8,128)(2,1)S(1)} %collective-permute-done), channel_id=1, source_target_pairs={{0,1},{1,2},{2,3},{3,4},{4,5},{5,6},{6,7},{8,9},{9,10},{10,11},{11... | collective-permute-start | bytes 786440 | tf_op jit(solution)/shard_map/ppermute | solution.py:13
  243.5 8.6 %collective-permute-start.2 = (bf16[2,2,256,128]{2,3,1,0:T(8,128)(2,1)S(1)}, bf16[2,2,256,128]{2,3,1,0:T(8,128)(2,1)S(1)}, u32[]{:S(2)}, u32[]{:S(2)}) collective-permute-start(bf16[2,2,256,128]{2,3,1,0:T(8,128)(2,1)S(1)} %collective-permute-done.1), channel_id=1, source_target_pairs={{0,1},{1,2},{2,3},{3,4},{4,5},{5,6},{6,7},{8,9},{9,10},{10,11},{11... | collective-permute-start | bytes 786440 | tf_op jit(solution)/shard_map/ppermute | solution.py:13
  252.1 37.8 %copy-start.3 = (bf16[2,2,256,128]{2,3,1,0:T(8,128)(2,1)}, bf16[2,2,256,128]{2,3,1,0:T(8,128)(2,1)S(1)}, u32[]{:S(2)}) copy-start(bf16[2,2,256,128]{2,3,1,0:T(8,128)(2,1)S(1)} %collective-permute-done.2) | copy-start | bytes 786436
  252.1 8.3 %collective-permute-start.3 = (bf16[2,2,256,128]{2,3,1,0:T(8,128)(2,1)S(1)}, bf16[2,2,256,128]{2,3,1,0:T(8,128)(2,1)S(1)}, u32[]{:S(2)}, u32[]{:S(2)}) collective-permute-start(bf16[2,2,256,128]{2,3,1,0:T(8,128)(2,1)S(1)} %collective-permute-done.2), channel_id=1, source_target_pairs={{0,1},{1,2},{2,3},{3,4},{4,5},{5,6},{6,7},{8,9},{9,10},{10,11},{11... | collective-permute-start | bytes 786440 | tf_op jit(solution)/shard_map/ppermute | solution.py:13
  260.3 8.4 %collective-permute-start.4 = (bf16[2,2,256,128]{2,3,1,0:T(8,128)(2,1)S(1)}, bf16[2,2,256,128]{2,3,1,0:T(8,128)(2,1)S(1)}, u32[]{:S(2)}, u32[]{:S(2)}) collective-permute-start(bf16[2,2,256,128]{2,3,1,0:T(8,128)(2,1)S(1)} %collective-permute-done.3), channel_id=1, source_target_pairs={{0,1},{1,2},{2,3},{3,4},{4,5},{5,6},{6,7},{8,9},{9,10},{10,11},{11... | collective-permute-start | bytes 786440 | tf_op jit(solution)/shard_map/ppermute | solution.py:13
  268.7 9.6 %collective-permute-start.5 = (bf16[2,2,256,128]{2,3,1,0:T(8,128)(2,1)S(1)}, bf16[2,2,256,128]{2,3,1,0:T(8,128)(2,1)S(1)}, u32[]{:S(2)}, u32[]{:S(2)}) collective-permute-start(bf16[2,2,256,128]{2,3,1,0:T(8,128)(2,1)S(1)} %collective-permute-done.4), channel_id=1, source_target_pairs={{0,1},{1,2},{2,3},{3,4},{4,5},{5,6},{6,7},{8,9},{9,10},{10,11},{11... | collective-permute-start | bytes 786440 | tf_op jit(solution)/shard_map/ppermute | solution.py:13
  278.4 10.4 %collective-permute-start.6 = (bf16[2,2,256,128]{2,3,1,0:T(8,128)(2,1)S(1)}, bf16[2,2,256,128]{2,3,1,0:T(8,128)(2,1)S(1)}, u32[]{:S(2)}, u32[]{:S(2)}) collective-permute-start(bf16[2,2,256,128]{2,3,1,0:T(8,128)(2,1)S(1)} %collective-permute-done.5), channel_id=1, source_target_pairs={{0,1},{1,2},{2,3},{3,4},{4,5},{5,6},{6,7},{8,9},{9,10},{10,11},{11... | collective-permute-start | bytes 786440 | tf_op jit(solution)/shard_map/ppermute | solution.py:13
  293.3 172.0 %copy-start.2 = (bf16[256,256]{1,0:T(8,128)(2,1)S(1)}, bf16[256,256]{1,0:T(8,128)(2,1)}, u32[]{:S(2)}) copy-start(bf16[256,256]{1,0:T(8,128)(2,1)} %param.8) | copy-start | bytes 393220
Sparse Core Ops, SparseCore 0:
  12.6 195.1 all-gather.1
  299.0 165.2 reduce-scatter.1
where the time goes:
time: 474 us; the launch traced here: 473 us
  waiting for transfers between devices  365 us (77%)
  starting transfers between devices  41.4 us (9%)
  matrix products  20.8 us (4%)
  local copies, waits for them, and re-layouts  18.6 us (4%)
  other arithmetic  13.8 us (3%)
  between operations  13.8 us (3%)
    reduce_scatter x1, waiting for transfers between devices, shards(): lax.psum_scatter(lax.dot_general(out_weight, attn_flat, (((0,), (1,)), ((...  165 us
    all_to_all x1, waiting for transfers between devices, shards(): lax.all_to_all(qkv_weight, 'fsdp', split_axis=1, concat_axis=0, tiled=True)  161 us
    ppermute x7, waiting for transfers between devices, from_behind(): return lax.ppermute(block, axis, route)  32.7 us
    ppermute x7, starting transfers between devices, from_behind(): return lax.ppermute(block, axis, route)  29.8 us
    all_to_all x1, starting transfers between devices, shards(): lax.all_to_all(qkv_weight, 'fsdp', split_axis=1, concat_axis=0, tiled=True)  11.6 us
  transfers between devices with their start and end apart: 10, of which 10 were waited for; matrix products, arithmetic and copies ran while one was open for 4% of the time, Pallas kernels for 0%

commit v1 on v0

--- a/solution.py
+++ b/solution.py
@@ -50,7 +50,10 @@
     var_rows = (picked_rows + change).astype(jnp.bfloat16)
     placed_rows = jnp.dot(placer, var_rows, preferred_element_type=jnp.float32).astype(jnp.bfloat16)
     variant = jnp.where(changed[:, None], placed_rows, hidden)
-    head_w = lax.all_to_all(qkv_weight, "fsdp", split_axis=1, concat_axis=0, tiled=True)
+    inter = lax.all_to_all(
+        jnp.stack(jnp.split(qkv_weight, lax.axis_size("fsdp"), axis=1)), "fsdp", 0, 0
+    )
+    head_w = jnp.concatenate(inter, axis=0)
     block_pos = my_block * tok_rows + jnp.arange(tok_rows)
 
     def finish(proj_rows, positions):

time: 474 us -> 488 us (1.030)
  local copies, waits for them, and re-layouts: 18.6 us -> 52 us
  waiting for transfers between devices: 365 us -> 352 us
  starting transfers between devices: 41.4 us -> 33.9 us
    all_to_all x1, waiting for transfers between devices: 161 us -> 34.6 us  [shards(): lax.all_to_all(jnp.stack(jnp.split(qkv_weight, lax.axis_size('fsdp'), axi...]
    all_gather x1, waiting for transfers between devices: 5.24 us -> 117 us  [shards(): lax.all_gather(dense_rows, 'fsdp', axis=1, tiled=True).astype(jnp.float32)]
    unnamed x11 -> x37, local copies, waits for them, and re-layouts: 9.09 us -> 50.4 us
    all_to_all x1 -> x0, local copies, waits for them, and re-layouts: 8.64 us -> none  [shards(): lax.all_to_all(qkv_weight, 'fsdp', split_axis=1, concat_axis=0, tiled=True)]
    ppermute x7, starting transfers between devices: 29.8 us -> 22.3 us  [from_behind(): return lax.ppermute(block, axis, route)]
    ppermute x7, waiting for transfers between devices: 32.7 us -> 40 us  [from_behind(): return lax.ppermute(block, axis, route)]
    reduce_scatter x1, waiting for transfers between devices: 165 us -> 160 us  [shards(): lax.psum_scatter(lax.dot_general(out_weight, attn_flat, (((0,), (1,)), ((...]
  transfers between devices with their start and end apart: 10 -> 10, of which waited for: 10 -> 10; matrix products, arithmetic and copies ran while one was open for 4% -> 12% of each run, Pallas kernels for 0% -> 0%
where the time goes in v1:
time: 488 us; the launch traced here: 487 us
  waiting for transfers between devices  352 us (72%)
  local copies, waits for them, and re-layouts  52 us (11%)
  starting transfers between devices  33.9 us (7%)
  matrix products  21.6 us (4%)
  between operations  13.8 us (3%)
  other arithmetic  13.6 us (3%)
    reduce_scatter x1, waiting for transfers between devices, shards(): lax.psum_scatter(lax.dot_general(out_weight, attn_flat, (((0,), (1,)), ((...  160 us
    all_gather x1, waiting for transfers between devices, shards(): lax.all_gather(dense_rows, 'fsdp', axis=1, tiled=True).astype(jnp.float32)  117 us
    unnamed x37, local copies, waits for them, and re-layouts  50.4 us
    ppermute x7, waiting for transfers between devices, from_behind(): return lax.ppermute(block, axis, route)  40 us
    all_to_all x1, waiting for transfers between devices, shards(): lax.all_to_all(jnp.stack(jnp.split(qkv_weight, lax.axis_size('fsdp'), axi...  34.6 us
    ppermute x7, starting transfers between devices, from_behind(): return lax.ppermute(block, axis, route)  22.3 us
    all_to_all x1, starting transfers between devices, shards(): lax.all_to_all(jnp.stack(jnp.split(qkv_weight, lax.axis_size('fsdp'), axi...  11.6 us
  transfers between devices with their start and end apart: 10, of which 10 were waited for; matrix products, arithmetic and copies ran while one was open for 12% of the time, Pallas kernels for 0%

profile of v1, /device:TPU:8, one launch (start us, length us, event | category | flops | bytes accessed | tf_op | source)
XLA Modules:
  0.0 486.6 jit_solution(11250850453023393324)
XLA Ops:
  6.5 0.8 broadcast_subtract_fusion
  7.4 1.1 fusion.105
  8.5 0.9 select_reduce_fusion
  9.4 1.4 fusion.26
  10.8 1.6 pad_maximum_fusion
  12.5 1.6 bitcast_dynamic-update-slice_fusion.31
  14.1 1.6 bitcast_dynamic-update-slice_fusion.30
  15.7 1.6 bitcast_dynamic-update-slice_fusion.29
  17.3 1.6 bitcast_dynamic-update-slice_fusion.28
  19.0 1.6 bitcast_dynamic-update-slice_fusion.27
  20.6 1.6 bitcast_dynamic-update-slice_fusion.26
  22.2 1.6 bitcast_dynamic-update-slice_fusion.25
  23.8 1.6 bitcast_dynamic-update-slice_fusion.24
  25.5 1.6 bitcast_dynamic-update-slice_fusion.23
  27.1 1.6 bitcast_dynamic-update-slice_fusion.22
  28.7 1.7 bitcast_dynamic-update-slice_fusion.21
  30.4 1.6 bitcast_dynamic-update-slice_fusion.20
  32.0 1.6 bitcast_dynamic-update-slice_fusion.19
  33.6 1.6 bitcast_dynamic-update-slice_fusion.18
  35.2 1.6 bitcast_dynamic-update-slice_fusion.17
  36.9 1.6 bitcast_dynamic-update-slice_fusion.16
  38.5 1.6 bitcast_dynamic-update-slice_fusion.15
  40.1 1.6 bitcast_dynamic-update-slice_fusion.14
  41.7 1.6 bitcast_dynamic-update-slice_fusion.13
  43.4 1.6 bitcast_dynamic-update-slice_fusion.12
  45.0 1.6 bitcast_dynamic-update-slice_fusion.11
  46.6 1.6 bitcast_dynamic-update-slice_fusion.10
  48.2 1.6 bitcast_dynamic-update-slice_fusion.9
  49.9 1.6 bitcast_dynamic-update-slice_fusion.8
  51.5 1.6 bitcast_dynamic-update-slice_fusion.7
  53.1 1.6 bitcast_dynamic-update-slice_fusion.6
  54.7 1.6 bitcast_dynamic-update-slice_fusion.5
  56.4 1.6 bitcast_dynamic-update-slice_fusion.4
  58.0 1.6 bitcast_dynamic-update-slice_fusion.3
  59.6 1.6 bitcast_dynamic-update-slice_fusion.2
  61.2 1.6 bitcast_dynamic-update-slice_fusion.1
  62.8 1.6 bitcast_dynamic-update-slice_fusion
  64.5 11.6 %all-to-all-start = ((bf16[32,256,384]{2,1,0:T(8,128)(2,1)}), bf16[32,256,384]{2,1,0:T(8,128)(2,1)}, u32[]{:S(2)}, u32[]{:S(2)}) async-start(bf16[32,256,384]{2,1,0:T(8,128)(2,1)} %bitcast_dynamic-update-slice_fusion), calls=%async_computation | async-start | bytes 12582912 | tf_op jit(solution)/shard_map/all_to_all | solution.py:53
  76.2 117.0 %all-gather.2.cloned.1.call-done = bf16[512,8192]{1,0:T(8,128)(2,1)} async-done(((bf16[512,256]{1,0:T(8,128)(2,1)}), bf16[512,8192]{1,0:T(8,128)(2,1)}) %all-gather.2.cloned.1.call-update) | async-done | bytes 8388624 | tf_op jit(solution)/shard_map/all_gather | solution.py:68
  193.1 5.1 %fusion.1 = f32[512]{0:T(512)S(1)} fusion(bf16[512,8192]{1,0:T(8,128)(2,1)} %all-gather.2.cloned.1.call-done), kind=kLoop, calls=%fused_computation.3 | loop fusion | flops 12582400 | bytes 8390656 | tf_op jit(solution)/shard_map/reduce_sum | solution.py:71
  198.2 34.6 %all-to-all-done = bf16[32,256,384]{2,1,0:T(8,128)(2,1)} async-done(((bf16[32,256,384]{2,1,0:T(8,128)(2,1)}), bf16[32,256,384]{2,1,0:T(8,128)(2,1)}, u32[]{:S(2)}, u32[]{:S(2)}) %all-to-all-start) | async-done | bytes 6291488 | tf_op jit(solution)/shard_map/all_to_all | solution.py:53
  232.9 8.8 %fusion.113 = (bf16[512,384]{0,1:T(8,128)(2,1)S(1)}, f32[512,384]{0,1:T(8,128)S(1)}) fusion(f32[512]{0:T(512)S(1)} %add_rsqrt_fusion, bf16[8192,384]{1,0:T(8,128)(2,1)} %bitcast.34, bf16[512,8192]{1,0:T(8,128)(2,1)} %all-gather.2.cloned.1.call-done, f32[8192]{0:T(1024)S(1)} %convert_element_type.105), kind=kOutput, calls=%fused_computation.232 | convolution fusion | flops 3234201600 | bytes 15894528 | tf_op jit(solution)/shard_map/dot_general | solution.py:70
  242.0 0.3 constant_dynamic-update-slice_fusion.8
  242.3 0.3 constant_dynamic-update-slice_fusion.7
  243.0 0.3 constant_dynamic-update-slice_fusion.6
  243.7 3.4 collective-permute-start
  247.1 4.9 %collective-permute-done = bf16[2,2,256,128]{2,3,1,0:T(8,128)(2,1)S(1)} collective-permute-done((bf16[2,2,256,128]{2,3,1,0:T(8,128)(2,1)S(1)}, bf16[2,2,256,128]{2,3,1,0:T(8,128)(2,1)S(1)}, u32[]{:S(2)}, u32[]{:S(2)}) %collective-permute-start) | collective-permute-done | bytes 262176 | tf_op jit(solution)/shard_map/ppermute | solution.py:13
  252.0 3.5 collective-permute-start.1
  255.5 4.7 collective-permute-done.1
  260.2 3.5 collective-permute-start.2
  263.8 5.5 %collective-permute-done.2 = bf16[2,2,256,128]{2,3,1,0:T(8,128)(2,1)S(1)} collective-permute-done((bf16[2,2,256,128]{2,3,1,0:T(8,128)(2,1)S(1)}, bf16[2,2,256,128]{2,3,1,0:T(8,128)(2,1)S(1)}, u32[]{:S(2)}, u32[]{:S(2)}) %collective-permute-start.2) | collective-permute-done | bytes 262176 | tf_op jit(solution)/shard_map/ppermute | solution.py:13
  269.3 3.1 collective-permute-start.3
  272.4 0.6 compare_and_fusion.6
  273.2 6.3 %collective-permute-done.3 = bf16[2,2,256,128]{2,3,1,0:T(8,128)(2,1)S(1)} collective-permute-done((bf16[2,2,256,128]{2,3,1,0:T(8,128)(2,1)S(1)}, bf16[2,2,256,128]{2,3,1,0:T(8,128)(2,1)S(1)}, u32[]{:S(2)}, u32[]{:S(2)}) %collective-permute-start.3) | collective-permute-done | bytes 262176 | tf_op jit(solution)/shard_map/ppermute | solution.py:13
  279.5 2.0 collective-permute-start.4
  282.1 8.2 %collective-permute-done.4 = bf16[2,2,256,128]{2,3,1,0:T(8,128)(2,1)S(1)} collective-permute-done((bf16[2,2,256,128]{2,3,1,0:T(8,128)(2,1)S(1)}, bf16[2,2,256,128]{2,3,1,0:T(8,128)(2,1)S(1)}, u32[]{:S(2)}, u32[]{:S(2)}) %collective-permute-start.4) | collective-permute-done | bytes 262176 | tf_op jit(solution)/shard_map/ppermute | solution.py:13
  290.3 2.0 collective-permute-start.5
  292.8 7.3 %collective-permute-done.5 = bf16[2,2,256,128]{2,3,1,0:T(8,128)(2,1)S(1)} collective-permute-done((bf16[2,2,256,128]{2,3,1,0:T(8,128)(2,1)S(1)}, bf16[2,2,256,128]{2,3,1,0:T(8,128)(2,1)S(1)}, u32[]{:S(2)}, u32[]{:S(2)}) %collective-permute-start.5) | collective-permute-done | bytes 262176 | tf_op jit(solution)/shard_map/ppermute | solution.py:13
  300.2 4.8 collective-permute-start.6
  305.6 3.1 collective-permute-done.6
  312.3 5.6 %fusion.2 = bf16[8192,512]{0,1:T(8,128)(2,1)} fusion(bf16[512,128]{1,0:T(8,128)(2,1)S(1)} %bitcast.173, bf16[128,8192]{1,0:T(8,128)(2,1)S(1)} %copy-done), kind=kOutput, calls=%fused_computation.5 | convolution fusion | flops 1077936128 | bytes 10616832 | tf_op jit(solution)/shard_map/dot_general | solution.py:115
  317.9 160.1 %reduce-scatter.2.cloned.1.call-done = bf16[256,512]{0,1:T(8,128)(2,1)} async-done(((bf16[8192,512]{0,1:T(8,128)(2,1)}), bf16[256,512]{0,1:T(8,128)(2,1)}) %reduce-scatter.2.cloned.1.call-update) | async-done | bytes 262160 | tf_op jit(solution)/shard_map/reduce_scatter | solution.py:114
  478.0 1.0 reshape.675
  479.0 0.8 add_convert_fusion
  (57 shorter events, 6.8 us)
Async XLA Ops:
  6.5 305.8 %copy-start = (bf16[128,8192]{1,0:T(8,128)(2,1)S(1)}, bf16[128,8192]{1,0:T(8,128)(2,1)}, u32[]{:S(2)}) copy-start(bf16[128,8192]{1,0:T(8,128)(2,1)} %param.12) | copy-start | bytes 6291460
  6.5 186.6 %all-gather.2.cloned.1.call-start = ((), (), s32[]{:S(2)}) async-start(), calls=%async_computation.2 | async-start | bytes 8650752 | tf_op jit(solution)/shard_map/all_gather | solution.py:68
  64.5 11.6 %copy-start.2 = (bf16[8192]{0:T(1024)(128)(2,1)S(1)}, bf16[8192]{0:T(1024)(128)(2,1)}, u32[]{:S(2)}) copy-start(bf16[8192]{0:T(1024)(128)(2,1)} %param.9) | copy-start | bytes 49156
  64.5 168.4 %all-to-all-start = ((bf16[32,256,384]{2,1,0:T(8,128)(2,1)}), bf16[32,256,384]{2,1,0:T(8,128)(2,1)}, u32[]{:S(2)}, u32[]{:S(2)}) async-start(bf16[32,256,384]{2,1,0:T(8,128)(2,1)} %bitcast_dynamic-update-slice_fusion), calls=%async_computation | async-start | bytes 12582912 | tf_op jit(solution)/shard_map/all_to_all | solution.py:53
  76.1 402.0 %reduce-scatter.2.cloned.1.call-start = ((), (), s32[]{:S(2)}) async-start(), calls=%async_computation.3 | async-start | bytes 8650752 | tf_op jit(solution)/shard_map/reduce_scatter | solution.py:114
  243.7 8.3 %collective-permute-start = (bf16[2,2,256,128]{2,3,1,0:T(8,128)(2,1)S(1)}, bf16[2,2,256,128]{2,3,1,0:T(8,128)(2,1)S(1)}, u32[]{:S(2)}, u32[]{:S(2)}) collective-permute-start(bf16[2,2,256,128]{2,3,1,0:T(8,128)(2,1)S(1)} %pad_maximum_fusion.1), channel_id=1, source_target_pairs={{0,1},{1,2},{2,3},{3,4},{4,5},{5,6},{6,7},{8,9},{9,10},{10,11},{11... | collective-permute-start | bytes 786440 | tf_op jit(solution)/shard_map/ppermute | solution.py:13
  252.0 8.3 %collective-permute-start.1 = (bf16[2,2,256,128]{2,3,1,0:T(8,128)(2,1)S(1)}, bf16[2,2,256,128]{2,3,1,0:T(8,128)(2,1)S(1)}, u32[]{:S(2)}, u32[]{:S(2)}) collective-permute-start(bf16[2,2,256,128]{2,3,1,0:T(8,128)(2,1)S(1)} %collective-permute-done), channel_id=1, source_target_pairs={{0,1},{1,2},{2,3},{3,4},{4,5},{5,6},{6,7},{8,9},{9,10},{10,11},{11... | collective-permute-start | bytes 786440 | tf_op jit(solution)/shard_map/ppermute | solution.py:13
  260.2 9.0 %collective-permute-start.2 = (bf16[2,2,256,128]{2,3,1,0:T(8,128)(2,1)S(1)}, bf16[2,2,256,128]{2,3,1,0:T(8,128)(2,1)S(1)}, u32[]{:S(2)}, u32[]{:S(2)}) collective-permute-start(bf16[2,2,256,128]{2,3,1,0:T(8,128)(2,1)S(1)} %collective-permute-done.1), channel_id=1, source_target_pairs={{0,1},{1,2},{2,3},{3,4},{4,5},{5,6},{6,7},{8,9},{9,10},{10,11},{11... | collective-permute-start | bytes 786440 | tf_op jit(solution)/shard_map/ppermute | solution.py:13
  269.3 10.2 %collective-permute-start.3 = (bf16[2,2,256,128]{2,3,1,0:T(8,128)(2,1)S(1)}, bf16[2,2,256,128]{2,3,1,0:T(8,128)(2,1)S(1)}, u32[]{:S(2)}, u32[]{:S(2)}) collective-permute-start(bf16[2,2,256,128]{2,3,1,0:T(8,128)(2,1)S(1)} %collective-permute-done.2), channel_id=1, source_target_pairs={{0,1},{1,2},{2,3},{3,4},{4,5},{5,6},{6,7},{8,9},{9,10},{10,11},{11... | collective-permute-start | bytes 786440 | tf_op jit(solution)/shard_map/ppermute | solution.py:13
  279.5 10.8 %collective-permute-start.4 = (bf16[2,2,256,128]{2,3,1,0:T(8,128)(2,1)S(1)}, bf16[2,2,256,128]{2,3,1,0:T(8,128)(2,1)S(1)}, u32[]{:S(2)}, u32[]{:S(2)}) collective-permute-start(bf16[2,2,256,128]{2,3,1,0:T(8,128)(2,1)S(1)} %collective-permute-done.3), channel_id=1, source_target_pairs={{0,1},{1,2},{2,3},{3,4},{4,5},{5,6},{6,7},{8,9},{9,10},{10,11},{11... | collective-permute-start | bytes 786440 | tf_op jit(solution)/shard_map/ppermute | solution.py:13
  290.3 9.9 %collective-permute-start.5 = (bf16[2,2,256,128]{2,3,1,0:T(8,128)(2,1)S(1)}, bf16[2,2,256,128]{2,3,1,0:T(8,128)(2,1)S(1)}, u32[]{:S(2)}, u32[]{:S(2)}) collective-permute-start(bf16[2,2,256,128]{2,3,1,0:T(8,128)(2,1)S(1)} %collective-permute-done.4), channel_id=1, source_target_pairs={{0,1},{1,2},{2,3},{3,4},{4,5},{5,6},{6,7},{8,9},{9,10},{10,11},{11... | collective-permute-start | bytes 786440 | tf_op jit(solution)/shard_map/ppermute | solution.py:13
  300.2 8.5 %collective-permute-start.6 = (bf16[2,2,256,128]{2,3,1,0:T(8,128)(2,1)S(1)}, bf16[2,2,256,128]{2,3,1,0:T(8,128)(2,1)S(1)}, u32[]{:S(2)}, u32[]{:S(2)}) collective-permute-start(bf16[2,2,256,128]{2,3,1,0:T(8,128)(2,1)S(1)} %collective-permute-done.5), channel_id=1, source_target_pairs={{0,1},{1,2},{2,3},{3,4},{4,5},{5,6},{6,7},{8,9},{9,10},{10,11},{11... | collective-permute-start | bytes 786440 | tf_op jit(solution)/shard_map/ppermute | solution.py:13
  317.9 161.1 %copy-start.1 = (bf16[256,256]{1,0:T(8,128)(2,1)S(1)}, bf16[256,256]{1,0:T(8,128)(2,1)}, u32[]{:S(2)}) copy-start(bf16[256,256]{1,0:T(8,128)(2,1)} %param.8) | copy-start | bytes 393220
Sparse Core Ops, SparseCore 0:
  12.6 180.5 all-gather.1
  318.0 159.9 reduce-scatter.1
